TPU v7x, 256 devices: a whole 4x4x8 slice. The times are simulated.
256 devices in a mesh: fsdp: 32 (over y, x, core), tp: 8 (over z).
Axes of the slice: x: 4, y: 4, z: 8, core: 2. Of those that a mesh axis runs over, the one named last changes fastest.
Arguments:
- learner_flat: bfloat16 [2, 159383552], P(None, ('fsdp', 'tp')), may hold values from -1.796875 to 1.796875
- param_offsets: int32 [2, 128, 4], replicated, may hold values from 0 to 622336, as said below
- owner_map: int32 [2, 128], replicated, may hold values from 0 to 31, as said below
- slice_map: int32 [32, 8], replicated, may hold values from 0 to 7, each once within a row
Outputs:
- query_absorbed: bfloat16 [2, 128, 1536, 512], P(None, 'fsdp', 'tp')
- output_absorbed: bfloat16 [2, 128, 7168, 512], P(None, 'fsdp', 'tp')
Inputs may be any that keep to these rules, and one draw needn't show every extreme that they name: `param_offsets`: in each layer the pieces of all heads' four parameters lie in a rank's 622592 entries one after another in some order, without gaps or intersections; a piece of a parameter holds that parameter's entries divided by 256; the last piece of each layer is a key up-projection piece. `owner_map`: in each layer every index of fsdp owns exactly 4 heads.
All inputs are finite; a program needn't handle non-finite values.
Results may differ from a plain program's by a relative error of at most 0.001.
Values may be sent and summed in bfloat16 or wider, within the bound.
A program may use at most 64 MiB of HBM per device.

v0:
```python
import math
import jax
import jax.numpy as jnp
from jax import lax
from jax.sharding import PartitionSpec as P

D = 7168
QR = 1536
KVR = 512
QK_NOPE = 128
V_DIM = 128


def for_sending(shard):
    return jax.tree.map(lambda a: a.astype(jnp.bfloat16) if a.dtype == jnp.float32 else a, shard)


def head_order(owner_map, per_group):
    head_count = owner_map.shape[1]
    head_index = jnp.arange(head_count, dtype=jnp.int32)
    same_owner = owner_map[:, :, None] == owner_map[:, None, :]
    before = head_index[None, None, :] < head_index[None, :, None]
    head_rank = jnp.sum(jnp.logical_and(same_owner, before).astype(jnp.int32), axis=2)
    head_slot = owner_map * per_group + head_rank
    slot_hits = head_slot[:, :, None] == head_index[None, None, :]
    return jnp.sum(jnp.where(slot_hits, head_index[None, :, None], 0), axis=1)


def cut_pieces(local_flat, begins, width_now, granule):
    layer_count, heads_here = begins.shape
    row_table = local_flat.reshape(layer_count, local_flat.shape[1] // granule, granule)
    row_steps = jnp.arange(width_now // granule, dtype=jnp.int32)
    row_ids = (begins[:, :, None] // granule + row_steps[None, None, :]).reshape(
        layer_count, heads_here * (width_now // granule)
    )
    picked = jnp.take_along_axis(row_table, row_ids[:, :, None], axis=1)
    return picked.reshape(layer_count, heads_here, width_now)


def refresh(local_flat, param_offsets, head_at, slice_row):
    fsdp_ways = lax.axis_size("fsdp")
    tensor_ways = lax.axis_size("tp")
    rank_total = fsdp_ways * tensor_ways
    layer_count = local_flat.shape[0]
    per_group = head_at.shape[1] // fsdp_ways
    widths = (
        QR * QK_NOPE // rank_total,
        QK_NOPE * KVR // rank_total,
        V_DIM * KVR // rank_total,
        D * V_DIM // rank_total,
    )
    granule = math.gcd(math.gcd(widths[0], widths[1]), math.gcd(widths[2], widths[3]))
    begins = jnp.take_along_axis(param_offsets, head_at[:, :, None], axis=1)
    pieces = tuple(
        (
            cut_pieces(local_flat, begins[:, :, kind_id], widths[kind_id], granule).reshape(
                layer_count, fsdp_ways, per_group, 1, widths[kind_id]
            )
            for kind_id in range(4)
        )
    )
    arrived = jax.tree.map(
        lambda part, own: part.astype(own.dtype),
        lax.all_to_all(for_sending(pieces), "fsdp", split_axis=1, concat_axis=3, tiled=True),
        pieces,
    )
    query_part, key_part, value_part, out_part = tuple(
        (
            arrived[kind_id].reshape(layer_count, per_group, fsdp_ways, 1, widths[kind_id])
            for kind_id in range(4)
        )
    )
    slice_query = QR // tensor_ways
    slice_output = D // tensor_ways
    blocks = fsdp_ways // tensor_ways

    def to_send(part_in, width_now):
        grouped = part_in.reshape(layer_count, per_group, tensor_ways, blocks, width_now)
        return jnp.take(grouped, slice_row, axis=2).reshape(
            layer_count, per_group, tensor_ways, blocks, 1, width_now
        )

    query_rows, out_rows = (
        lax.all_to_all(
            to_send(query_part, widths[0]), "tp", split_axis=2, concat_axis=4, tiled=True
        ),
        lax.all_to_all(to_send(out_part, widths[3]), "tp", split_axis=2, concat_axis=4, tiled=True),
    )
    query_rows = query_rows.reshape(layer_count, per_group, slice_query, QK_NOPE)
    out_rows = out_rows.reshape(layer_count, per_group, slice_output, V_DIM)
    key_full, value_full = (
        lax.all_gather(key_part, "tp", axis=3, tiled=True),
        lax.all_gather(value_part, "tp", axis=3, tiled=True),
    )
    key_full = key_full.reshape(layer_count, per_group, QK_NOPE, KVR)
    value_full = value_full.reshape(layer_count, per_group, V_DIM, KVR)
    query_absorbed = jnp.einsum(
        "lhrc,lhck->lhrk", query_rows, key_full, preferred_element_type=jnp.float32
    ).astype(jnp.bfloat16)
    output_absorbed = jnp.einsum(
        "lhrc,lhck->lhrk", out_rows, value_full, preferred_element_type=jnp.float32
    ).astype(jnp.bfloat16)
    return (query_absorbed, output_absorbed)


def per_device(learner_flat, param_offsets, owner_map, slice_map):
    fsdp_ways = lax.axis_size("fsdp")
    per_group = owner_map.shape[1] // fsdp_ways
    head_at = head_order(owner_map, per_group)
    slice_row = lax.dynamic_index_in_dim(slice_map, lax.axis_index("fsdp"), 0, keepdims=False)
    layer_results = [
        refresh(
            learner_flat[layer_id : layer_id + 1],
            param_offsets[layer_id : layer_id + 1],
            head_at[layer_id : layer_id + 1],
            slice_row,
        )
        for layer_id in range(learner_flat.shape[0])
    ]
    query_absorbed = jnp.concatenate([result_pair[0] for result_pair in layer_results], axis=0)
    output_absorbed = jnp.concatenate([result_pair[1] for result_pair in layer_results], axis=0)
    return (query_absorbed, output_absorbed)


def solution(mesh):
    placed = (P(None, ("fsdp", "tp")), P(), P(), P())
    return jax.shard_map(
        per_device,
        mesh=mesh,
        in_specs=placed,
        out_specs=(P(None, "fsdp", "tp", None), P(None, "fsdp", "tp", None)),
        check_vma=False,
    )
```

profile of v0, /device:TPU:38, one launch (start us, length us, event | category | flops | bytes accessed | tf_op | source)
XLA Modules:
  0.0 371.7 jit_solution(2697430013469942218)
XLA Ops:
  4.4 28.8 %slice_reduce_fusion.1 = (bf16[622592]{0:T(1024)(128)(2,1)S(1)}, bf16[622592]{0:T(1024)(128)(2,1)}) fusion(bf16[2,622592]{1,0:T(2,128)(2,1)} %param.16), kind=kLoop, calls=%fused_computation.18 | loop fusion | bytes 4980736 | tf_op jit(solution)/shard_map/slice | solution.py:113
  35.2 7.6 %all-to-all-start.8 = ((bf16[1,32,4,1,256]{4,2,3,0,1:T(4,128)(2,1)}), bf16[1,32,4,1,256]{4,2,3,0,1:T(4,128)(2,1)S(1)}, u32[]{:S(2)}, u32[]{:S(2)}) async-start(bf16[1,32,4,1,256]{4,2,3,0,1:T(4,128)(2,1)} %bitcast.57), calls=%async_computation.8 | async-start | bytes 131072 | tf_op jit(solution)/shard_map/all_to_all | solution.py:64
  46.9 2.1 gather_fusion.1
  48.9 2.2 reshape.662
  55.8 7.4 %all-to-all-start.2 = ((bf16[1,32,4,1,256]{4,2,3,0,1:T(4,128)(2,1)}), bf16[1,32,4,1,256]{4,2,3,0,1:T(4,128)(2,1)S(1)}, u32[]{:S(2)}, u32[]{:S(2)}) async-start(bf16[1,32,4,1,256]{4,2,3,0,1:T(4,128)(2,1)} %bitcast.18), calls=%async_computation.2 | async-start | bytes 131072 | tf_op jit(solution)/shard_map/all_to_all | solution.py:64
  65.1 3.8 %all-to-all-done.2 = bf16[1,32,4,1,256]{4,2,3,0,1:T(4,128)(2,1)S(1)} async-done(((bf16[1,32,4,1,256]{4,2,3,0,1:T(4,128)(2,1)}), bf16[1,32,4,1,256]{4,2,3,0,1:T(4,128)(2,1)S(1)}, u32[]{:S(2)}, u32[]{:S(2)}) %all-to-all-start.2) | async-done | bytes 65568 | tf_op jit(solution)/shard_map/all_to_all | solution.py:64
  68.9 6.2 %all-to-all-start.11 = ((bf16[1,32,4,1,256]{4,2,3,0,1:T(4,128)(2,1)}), bf16[1,32,4,1,256]{4,2,3,0,1:T(4,128)(2,1)}, u32[]{:S(2)}, u32[]{:S(2)}) async-start(bf16[1,32,4,1,256]{4,2,3,0,1:T(4,128)(2,1)} %bitcast.74), calls=%async_computation.11 | async-start | bytes 131072 | tf_op jit(solution)/shard_map/all_to_all | solution.py:64
  75.1 5.5 %gather_fusion.8 = bf16[1792,256]{1,0:T(8,128)(2,1)S(1)} fusion(bf16[2432,256]{1,0:T(8,128)(2,1)S(1)} %reshape.643, s32[2048]{0:T(1024)S(1)} %pad_clamp_fusion.1), kind=kCustom, calls=%fused_computation.4.clone | custom fusion | bytes 1842176 | tf_op jit(solution)/shard_map/jit(take_along_axis)/gather | solution.py:36
  83.8 7.5 %all-to-all-start.5 = ((bf16[1,32,4,1,256]{4,2,3,0,1:T(4,128)(2,1)}), bf16[1,32,4,1,256]{4,2,3,0,1:T(4,128)(2,1)S(1)}, u32[]{:S(2)}, u32[]{:S(2)}) async-start(bf16[1,32,4,1,256]{4,2,3,0,1:T(4,128)(2,1)} %bitcast.40), calls=%async_computation.5 | async-start | bytes 131072 | tf_op jit(solution)/shard_map/all_to_all | solution.py:64
  91.3 2.1 gather_fusion.5
  93.4 3.6 all-to-all-done.5
  97.6 5.6 %all-to-all-start = ((bf16[1,32,4,1,768]{4,2,3,0,1:T(4,128)(2,1)}), bf16[1,32,4,1,768]{4,2,3,0,1:T(4,128)(2,1)S(1)}, u32[]{:S(2)}, u32[]{:S(2)}) async-start(bf16[1,32,4,1,768]{4,2,3,0,1:T(4,128)(2,1)} %bitcast.6), calls=%async_computation | async-start | bytes 393216 | tf_op jit(solution)/shard_map/all_to_all | solution.py:64
  104.1 5.7 %all-to-all-done = bf16[1,32,4,1,768]{4,2,3,0,1:T(4,128)(2,1)S(1)} async-done(((bf16[1,32,4,1,768]{4,2,3,0,1:T(4,128)(2,1)}), bf16[1,32,4,1,768]{4,2,3,0,1:T(4,128)(2,1)S(1)}, u32[]{:S(2)}, u32[]{:S(2)}) %all-to-all-start) | async-done | bytes 196640 | tf_op jit(solution)/shard_map/all_to_all | solution.py:64
  109.8 5.5 %all-to-all-start.3 = ((bf16[1,32,4,1,768]{4,2,3,0,1:T(4,128)(2,1)}), bf16[1,32,4,1,768]{4,2,3,0,1:T(4,128)(2,1)S(1)}, u32[]{:S(2)}, u32[]{:S(2)}) async-start(bf16[1,32,4,1,768]{4,2,3,0,1:T(4,128)(2,1)} %bitcast.28), calls=%async_computation.3 | async-start | bytes 393216 | tf_op jit(solution)/shard_map/all_to_all | solution.py:64
  116.9 4.9 %all-to-all-done.3 = bf16[1,32,4,1,768]{4,2,3,0,1:T(4,128)(2,1)S(1)} async-done(((bf16[1,32,4,1,768]{4,2,3,0,1:T(4,128)(2,1)}), bf16[1,32,4,1,768]{4,2,3,0,1:T(4,128)(2,1)S(1)}, u32[]{:S(2)}, u32[]{:S(2)}) %all-to-all-start.3) | async-done | bytes 196640 | tf_op jit(solution)/shard_map/all_to_all | solution.py:64
  121.9 5.5 %all-to-all-start.6 = ((bf16[1,32,4,1,3584]{4,2,3,0,1:T(4,128)(2,1)}), bf16[1,32,4,1,3584]{4,2,3,0,1:T(4,128)(2,1)S(1)}, u32[]{:S(2)}, u32[]{:S(2)}) async-start(bf16[1,32,4,1,3584]{4,2,3,0,1:T(4,128)(2,1)} %bitcast.45), calls=%async_computation.6 | async-start | bytes 1835008 | tf_op jit(solution)/shard_map/all_to_all | solution.py:64
  127.4 5.5 %gather_fusion.11 = bf16[1792,256]{1,0:T(8,128)(2,1)S(1)} fusion(bf16[2432,256]{1,0:T(8,128)(2,1)S(1)} %reshape.662, s32[2048]{0:T(1024)S(1)} %pad_clamp_fusion), kind=kCustom, calls=%fused_computation.12.clone | custom fusion | bytes 1842176 | tf_op jit(solution)/shard_map/jit(take_along_axis)/gather | solution.py:36
  134.5 6.2 %all-to-all-done.6 = bf16[1,32,4,1,3584]{4,2,3,0,1:T(4,128)(2,1)S(1)} async-done(((bf16[1,32,4,1,3584]{4,2,3,0,1:T(4,128)(2,1)}), bf16[1,32,4,1,3584]{4,2,3,0,1:T(4,128)(2,1)S(1)}, u32[]{:S(2)}, u32[]{:S(2)}) %all-to-all-start.6) | async-done | bytes 917536 | tf_op jit(solution)/shard_map/all_to_all | solution.py:64
  140.7 6.4 %all-to-all-start.9 = ((bf16[1,32,4,1,3584]{4,2,3,0,1:T(4,128)(2,1)}), bf16[1,32,4,1,3584]{4,2,3,0,1:T(4,128)(2,1)S(1)}, u32[]{:S(2)}, u32[]{:S(2)}) async-start(bf16[1,32,4,1,3584]{4,2,3,0,1:T(4,128)(2,1)} %bitcast.62), calls=%async_computation.9 | async-start | bytes 1835008 | tf_op jit(solution)/shard_map/all_to_all | solution.py:64
  149.9 10.5 %all-to-all-done.9 = bf16[1,32,4,1,3584]{4,2,3,0,1:T(4,128)(2,1)S(1)} async-done(((bf16[1,32,4,1,3584]{4,2,3,0,1:T(4,128)(2,1)}), bf16[1,32,4,1,3584]{4,2,3,0,1:T(4,128)(2,1)S(1)}, u32[]{:S(2)}, u32[]{:S(2)}) %all-to-all-start.9) | async-done | bytes 917536 | tf_op jit(solution)/shard_map/all_to_all | solution.py:64
  160.4 8.6 %all-to-all-start.1 = ((bf16[1,4,8,4,1,768]{5,3,1,4,0,2:T(4,128)(2,1)}), bf16[1,4,8,4,1,768]{5,3,1,4,0,2:T(4,128)(2,1)S(1)}, u32[]{:S(2)}, u32[]{:S(2)}) async-start(bf16[1,4,8,4,1,768]{5,3,1,4,0,2:T(4,128)(2,1)} %get-tuple-element.46), calls=%async_computation.1 | async-start | bytes 393216 | tf_op jit(solution)/shard_map/all_to_all | solution.py:84
  172.4 7.0 %all-to-all-done.1 = bf16[1,4,8,4,1,768]{5,3,1,4,0,2:T(4,128)(2,1)S(1)} async-done(((bf16[1,4,8,4,1,768]{5,3,1,4,0,2:T(4,128)(2,1)}), bf16[1,4,8,4,1,768]{5,3,1,4,0,2:T(4,128)(2,1)S(1)}, u32[]{:S(2)}, u32[]{:S(2)}) %all-to-all-start.1) | async-done | bytes 196640 | tf_op jit(solution)/shard_map/all_to_all | solution.py:84
  179.4 4.8 %all-to-all-start.4 = ((bf16[1,4,8,4,1,768]{5,3,1,4,0,2:T(4,128)(2,1)}), bf16[1,4,8,4,1,768]{5,3,1,4,0,2:T(4,128)(2,1)S(1)}, u32[]{:S(2)}, u32[]{:S(2)}) async-start(bf16[1,4,8,4,1,768]{5,3,1,4,0,2:T(4,128)(2,1)} %get-tuple-element.47), calls=%async_computation.4 | async-start | bytes 393216 | tf_op jit(solution)/shard_map/all_to_all | solution.py:84
  186.0 7.8 %all-to-all-done.4 = bf16[1,4,8,4,1,768]{5,3,1,4,0,2:T(4,128)(2,1)S(1)} async-done(((bf16[1,4,8,4,1,768]{5,3,1,4,0,2:T(4,128)(2,1)}), bf16[1,4,8,4,1,768]{5,3,1,4,0,2:T(4,128)(2,1)S(1)}, u32[]{:S(2)}, u32[]{:S(2)}) %all-to-all-start.4) | async-done | bytes 196640 | tf_op jit(solution)/shard_map/all_to_all | solution.py:84
  193.8 27.8 %all_to_all.180 = bf16[1,4,8,4,1,3584]{5,3,1,4,0,2:T(4,128)(2,1)S(1)} all-to-all(bf16[1,4,8,4,1,3584]{5,3,1,4,0,2:T(4,128)(2,1)S(1)} %get-tuple-element.44), channel_id=1, replica_groups=mesh['fsdp'=32,'tp'=8] {'tp'}, dimensions={2} | all-to-all | bytes 1835008 | tf_op jit(solution)/shard_map/all_to_all | solution.py:87
  221.6 4.9 %all-to-all-start.10 = ((bf16[1,4,8,4,1,3584]{5,3,1,4,0,2:T(4,128)(2,1)}), bf16[1,4,8,4,1,3584]{5,3,1,4,0,2:T(4,128)(2,1)S(1)}, u32[]{:S(2)}, u32[]{:S(2)}) async-start(bf16[1,4,8,4,1,3584]{5,3,1,4,0,2:T(4,128)(2,1)} %get-tuple-element.45), calls=%async_computation.10 | async-start | bytes 1835008 | tf_op jit(solution)/shard_map/all_to_all | solution.py:87
  226.5 41.6 %all-gather = bf16[1,1,4,32,8,256]{5,3,4,2,1,0:T(8,128)(2,1)S(1)} all-gather(bf16[1,1,4,32,1,256]{5,3,4,2,1,0:T(8,128)(2,1)S(1)} %bitcast.216), channel_id=2, replica_groups=mesh['fsdp'=32,'tp'=8] {'tp'}, dimensions={4}, use_global_device_ids=true | all-gather | bytes 589824 | tf_op jit(solution)/shard_map/all_gather | solution.py:92
  268.6 25.5 %all-gather.2 = bf16[1,1,4,32,8,256]{5,3,4,2,1,0:T(8,128)(2,1)S(1)} all-gather(bf16[1,1,4,32,1,256]{5,3,4,2,1,0:T(8,128)(2,1)S(1)} %bitcast.217), channel_id=4, replica_groups=mesh['fsdp'=32,'tp'=8] {'tp'}, dimensions={4}, use_global_device_ids=true | all-gather | bytes 589824 | tf_op jit(solution)/shard_map/all_gather | solution.py:93
  294.6 25.5 %all-gather.1 = bf16[1,1,4,32,8,256]{5,3,4,2,1,0:T(8,128)(2,1)S(1)} all-gather(bf16[1,1,4,32,1,256]{5,3,4,2,1,0:T(8,128)(2,1)S(1)} %bitcast.218), channel_id=3, replica_groups=mesh['fsdp'=32,'tp'=8] {'tp'}, dimensions={4}, use_global_device_ids=true | all-gather | bytes 589824 | tf_op jit(solution)/shard_map/all_gather | solution.py:92
  323.3 25.2 %all-gather.3 = bf16[1,1,4,32,8,256]{5,3,4,2,1,0:T(8,128)(2,1)S(1)} all-gather(bf16[1,1,4,32,1,256]{5,3,4,2,1,0:T(8,128)(2,1)S(1)} %bitcast.219), channel_id=5, replica_groups=mesh['fsdp'=32,'tp'=8] {'tp'}, dimensions={4}, use_global_device_ids=true | all-gather | bytes 589824 | tf_op jit(solution)/shard_map/all_gather | solution.py:93
  364.8 2.1 convert_bitcast_fusion
  368.1 3.7 pad_maximum_fusion
  (138 shorter events, 53.7 us)
Async XLA Ops:
  0.6 146.5 %copy-start = (s32[32,8]{0,1:T(8,128)S(1)}, s32[32,8]{0,1:T(8,128)}, u32[]{:S(2)}) copy-start(s32[32,8]{0,1:T(8,128)} %param.19) | copy-start | bytes 3076
  35.2 20.7 %all-to-all-start.8 = ((bf16[1,32,4,1,256]{4,2,3,0,1:T(4,128)(2,1)}), bf16[1,32,4,1,256]{4,2,3,0,1:T(4,128)(2,1)S(1)}, u32[]{:S(2)}, u32[]{:S(2)}) async-start(bf16[1,32,4,1,256]{4,2,3,0,1:T(4,128)(2,1)} %bitcast.57), calls=%async_computation.8 | async-start | bytes 131072 | tf_op jit(solution)/shard_map/all_to_all | solution.py:64
  55.8 13.1 %all-to-all-start.2 = ((bf16[1,32,4,1,256]{4,2,3,0,1:T(4,128)(2,1)}), bf16[1,32,4,1,256]{4,2,3,0,1:T(4,128)(2,1)S(1)}, u32[]{:S(2)}, u32[]{:S(2)}) async-start(bf16[1,32,4,1,256]{4,2,3,0,1:T(4,128)(2,1)} %bitcast.18), calls=%async_computation.2 | async-start | bytes 131072 | tf_op jit(solution)/shard_map/all_to_all | solution.py:64
  68.9 14.9 %all-to-all-start.11 = ((bf16[1,32,4,1,256]{4,2,3,0,1:T(4,128)(2,1)}), bf16[1,32,4,1,256]{4,2,3,0,1:T(4,128)(2,1)}, u32[]{:S(2)}, u32[]{:S(2)}) async-start(bf16[1,32,4,1,256]{4,2,3,0,1:T(4,128)(2,1)} %bitcast.74), calls=%async_computation.11 | async-start | bytes 131072 | tf_op jit(solution)/shard_map/all_to_all | solution.py:64
  80.6 22.6 %copy-start.13 = (pred[384]{0:T(512)(128)(4,1)S(1)}, pred[384]{0:T(512)(128)(4,1)}, u32[]{:S(2)}) copy-start(pred[384]{0:T(512)(128)(4,1)} %get-tuple-element.38) | copy-start | bytes 1156
  83.8 13.2 %all-to-all-start.5 = ((bf16[1,32,4,1,256]{4,2,3,0,1:T(4,128)(2,1)}), bf16[1,32,4,1,256]{4,2,3,0,1:T(4,128)(2,1)S(1)}, u32[]{:S(2)}, u32[]{:S(2)}) async-start(bf16[1,32,4,1,256]{4,2,3,0,1:T(4,128)(2,1)} %bitcast.40), calls=%async_computation.5 | async-start | bytes 131072 | tf_op jit(solution)/shard_map/all_to_all | solution.py:64
  91.3 24.0 %copy-start.12 = (pred[1792]{0:T(1024)(128)(4,1)S(1)}, pred[1792]{0:T(1024)(128)(4,1)}, u32[]{:S(2)}) copy-start(pred[1792]{0:T(1024)(128)(4,1)} %get-tuple-element.16) | copy-start | bytes 5380
  97.0 0.6 copy-start.8
  97.6 12.2 %all-to-all-start = ((bf16[1,32,4,1,768]{4,2,3,0,1:T(4,128)(2,1)}), bf16[1,32,4,1,768]{4,2,3,0,1:T(4,128)(2,1)S(1)}, u32[]{:S(2)}, u32[]{:S(2)}) async-start(bf16[1,32,4,1,768]{4,2,3,0,1:T(4,128)(2,1)} %bitcast.6), calls=%async_computation | async-start | bytes 393216 | tf_op jit(solution)/shard_map/all_to_all | solution.py:64
  109.8 5.5 %copy-start.1 = (bf16[1,32,4,1,768]{4,2,3,0,1:T(4,128)(2,1)}, bf16[1,32,4,1,768]{4,2,3,0,1:T(4,128)(2,1)S(1)}, u32[]{:S(2)}) copy-start(bf16[1,32,4,1,768]{4,2,3,0,1:T(4,128)(2,1)S(1)} %all-to-all-done) | copy-start | bytes 589828
  109.8 12.1 %all-to-all-start.3 = ((bf16[1,32,4,1,768]{4,2,3,0,1:T(4,128)(2,1)}), bf16[1,32,4,1,768]{4,2,3,0,1:T(4,128)(2,1)S(1)}, u32[]{:S(2)}, u32[]{:S(2)}) async-start(bf16[1,32,4,1,768]{4,2,3,0,1:T(4,128)(2,1)} %bitcast.28), calls=%async_computation.3 | async-start | bytes 393216 | tf_op jit(solution)/shard_map/all_to_all | solution.py:64
  115.6 11.7 %copy-start.10 = (s32[1,1792,1]{1,2,0:T(1,128)S(1)}, s32[1,1792,1]{1,2,0:T(1,128)}, u32[]{:S(2)}) copy-start(s32[1,1792,1]{1,2,0:T(1,128)} %get-tuple-element.35) | copy-start | bytes 21508
  121.9 11.0 %copy-start.4 = (bf16[1,32,4,1,768]{4,2,3,0,1:T(4,128)(2,1)}, bf16[1,32,4,1,768]{4,2,3,0,1:T(4,128)(2,1)S(1)}, u32[]{:S(2)}) copy-start(bf16[1,32,4,1,768]{4,2,3,0,1:T(4,128)(2,1)S(1)} %all-to-all-done.3) | copy-start | bytes 589828
  121.9 18.8 %all-to-all-start.6 = ((bf16[1,32,4,1,3584]{4,2,3,0,1:T(4,128)(2,1)}), bf16[1,32,4,1,3584]{4,2,3,0,1:T(4,128)(2,1)S(1)}, u32[]{:S(2)}, u32[]{:S(2)}) async-start(bf16[1,32,4,1,3584]{4,2,3,0,1:T(4,128)(2,1)} %bitcast.45), calls=%async_computation.6 | async-start | bytes 1835008 | tf_op jit(solution)/shard_map/all_to_all | solution.py:64
  127.4 5.5 %copy-start.11 = (pred[1792]{0:T(1024)(128)(4,1)S(1)}, pred[1792]{0:T(1024)(128)(4,1)}, u32[]{:S(2)}) copy-start(pred[1792]{0:T(1024)(128)(4,1)} %get-tuple-element.34) | copy-start | bytes 5380
  133.2 14.1 %copy-start.2 = (bf16[1,32,4,1,768]{4,2,3,0,1:T(4,128)(2,1)S(1)}, bf16[1,32,4,1,768]{4,2,3,0,1:T(4,128)(2,1)}, u32[]{:S(2)}) copy-start(bf16[1,32,4,1,768]{4,2,3,0,1:T(4,128)(2,1)} %copy-done.1) | copy-start | bytes 589828
  134.5 12.9 %copy-start.5 = (bf16[1,32,4,1,768]{4,2,3,0,1:T(4,128)(2,1)S(1)}, bf16[1,32,4,1,768]{4,2,3,0,1:T(4,128)(2,1)}, u32[]{:S(2)}) copy-start(bf16[1,32,4,1,768]{4,2,3,0,1:T(4,128)(2,1)} %copy-done.4) | copy-start | bytes 589828
  140.7 19.8 %all-to-all-start.9 = ((bf16[1,32,4,1,3584]{4,2,3,0,1:T(4,128)(2,1)}), bf16[1,32,4,1,3584]{4,2,3,0,1:T(4,128)(2,1)S(1)}, u32[]{:S(2)}, u32[]{:S(2)}) async-start(bf16[1,32,4,1,3584]{4,2,3,0,1:T(4,128)(2,1)} %bitcast.62), calls=%async_computation.9 | async-start | bytes 1835008 | tf_op jit(solution)/shard_map/all_to_all | solution.py:64
  160.4 19.0 %all-to-all-start.1 = ((bf16[1,4,8,4,1,768]{5,3,1,4,0,2:T(4,128)(2,1)}), bf16[1,4,8,4,1,768]{5,3,1,4,0,2:T(4,128)(2,1)S(1)}, u32[]{:S(2)}, u32[]{:S(2)}) async-start(bf16[1,4,8,4,1,768]{5,3,1,4,0,2:T(4,128)(2,1)} %get-tuple-element.46), calls=%async_computation.1 | async-start | bytes 393216 | tf_op jit(solution)/shard_map/all_to_all | solution.py:84
  179.4 6.6 %copy-start.3 = (bf16[1,4,8,4,1,768]{5,3,1,4,0,2:T(4,128)(2,1)}, bf16[1,4,8,4,1,768]{5,3,1,4,0,2:T(4,128)(2,1)S(1)}, u32[]{:S(2)}) copy-start(bf16[1,4,8,4,1,768]{5,3,1,4,0,2:T(4,128)(2,1)S(1)} %all-to-all-done.1) | copy-start | bytes 589828
  179.4 14.4 %all-to-all-start.4 = ((bf16[1,4,8,4,1,768]{5,3,1,4,0,2:T(4,128)(2,1)}), bf16[1,4,8,4,1,768]{5,3,1,4,0,2:T(4,128)(2,1)S(1)}, u32[]{:S(2)}, u32[]{:S(2)}) async-start(bf16[1,4,8,4,1,768]{5,3,1,4,0,2:T(4,128)(2,1)} %get-tuple-element.47), calls=%async_computation.4 | async-start | bytes 393216 | tf_op jit(solution)/shard_map/all_to_all | solution.py:84
  193.8 27.8 %copy-start.6 = (bf16[1,4,8,4,1,768]{5,3,1,4,0,2:T(4,128)(2,1)}, bf16[1,4,8,4,1,768]{5,3,1,4,0,2:T(4,128)(2,1)S(1)}, u32[]{:S(2)}) copy-start(bf16[1,4,8,4,1,768]{5,3,1,4,0,2:T(4,128)(2,1)S(1)} %all-to-all-done.4) | copy-start | bytes 589828
  221.6 141.6 %all-to-all-start.10 = ((bf16[1,4,8,4,1,3584]{5,3,1,4,0,2:T(4,128)(2,1)}), bf16[1,4,8,4,1,3584]{5,3,1,4,0,2:T(4,128)(2,1)S(1)}, u32[]{:S(2)}, u32[]{:S(2)}) async-start(bf16[1,4,8,4,1,3584]{5,3,1,4,0,2:T(4,128)(2,1)} %get-tuple-element.45), calls=%async_computation.10 | async-start | bytes 1835008 | tf_op jit(solution)/shard_map/all_to_all | solution.py:87
  268.6 26.0 %copy-start.9 = (bf16[1,32,4,1,256]{4,2,3,0,1:T(4,128)(2,1)S(1)}, bf16[1,32,4,1,256]{4,2,3,0,1:T(4,128)(2,1)}, u32[]{:S(2)}) copy-start(bf16[1,32,4,1,256]{4,2,3,0,1:T(4,128)(2,1)} %copy-done.8) | copy-start | bytes 196612
  358.5 1.3 copy-start.7
where the time goes:
time: 373 us; the launch traced here: 372 us
  blocking collectives  146 us (39%)
  local copies, waits for them, and re-layouts  85.3 us (23%)
  starting transfers between devices  69.7 us (19%)
  waiting for transfers between devices  49.5 us (13%)
  other arithmetic  15.4 us (4%)
  matrix products  4.9 us (1%)
    all_gather x2, blocking collectives, refresh(): lax.all_gather(key_part, 'tp', axis=3, tiled=True)  67.1 us
    all_to_all x8, starting transfers between devices, refresh(): lax.all_to_all(for_sending(pieces), 'fsdp', split_axis=1, concat_axis=3,...  51.5 us
    all_gather x2, blocking collectives, refresh(): lax.all_gather(value_part, 'tp', axis=3, tiled=True)  50.7 us
    all_to_all x8, waiting for transfers between devices, refresh(): lax.all_to_all(for_sending(pieces), 'fsdp', split_axis=1, concat_axis=3,...  34.7 us
    slice x1, local copies, waits for them, and re-layouts, per_device(): learner_flat[layer_id:layer_id + 1]  28.8 us
    all_to_all x1, blocking collectives, refresh(): lax.all_to_all(to_send(out_part, widths[3]), 'tp', split_axis=2, concat_a...  27.8 us
    gather x8, local copies, waits for them, and re-layouts, cut_pieces(): picked = jnp.take_along_axis(row_table, row_ids[:, :, None], axis=1)  18.4 us
    all_to_all x2, waiting for transfers between devices, refresh(): lax.all_to_all(to_send(query_part, widths[0]), 'tp', split_axis=2, concat...  14.8 us
  transfers between devices with their start and end apart: 11, of which 8 were waited for; matrix products, arithmetic and copies ran while one was open for 17% of the time, Pallas kernels for 0%

commit v1 on v0

--- a/solution.py
+++ b/solution.py
@@ -9,6 +9,12 @@
 KVR = 512
 QK_NOPE = 128
 V_DIM = 128
+
+
+def tiled_gather(x, axis, dim):
+    count = lax.axis_size(axis)
+    repeats = [count if d == dim else 1 for d in range(x.ndim)]
+    return lax.all_to_all(jnp.tile(x, repeats), axis, split_axis=dim, concat_axis=dim, tiled=True)
 
 
 def for_sending(shard):
@@ -90,7 +96,7 @@
     out_rows = out_rows.reshape(layer_count, per_group, slice_output, V_DIM)
     key_full, value_full = (
         lax.all_gather(key_part, "tp", axis=3, tiled=True),
-        lax.all_gather(value_part, "tp", axis=3, tiled=True),
+        tiled_gather(value_part, "tp", 3),
     )
     key_full = key_full.reshape(layer_count, per_group, QK_NOPE, KVR)
     value_full = value_full.reshape(layer_count, per_group, V_DIM, KVR)

time: 373 us -> 361 us (0.968)
  blocking collectives: 146 us -> 97 us
  waiting for transfers between devices: 49.5 us -> 81.4 us
  starting transfers between devices: 69.7 us -> 79.1 us
  local copies, waits for them, and re-layouts: 85.3 us -> 80 us
    all_gather x2 -> x0, blocking collectives: 50.7 us -> none  [refresh(): lax.all_gather(value_part, 'tp', axis=3, tiled=True)]
    all_to_all x0 -> x2, waiting for transfers between devices: none -> 28.8 us  [tiled_gather(): lax.all_to_all(jnp.tile(x, repeats), axis, split_axis=dim, concat_axis=di...]
    all_to_all x0 -> x2, starting transfers between devices: none -> 11.2 us  [tiled_gather(): lax.all_to_all(jnp.tile(x, repeats), axis, split_axis=dim, concat_axis=di...]
    all_to_all x8, waiting for transfers between devices: 34.7 us -> 44.2 us  [refresh(): lax.all_to_all(for_sending(pieces), 'fsdp', split_axis=1, concat_axis=3,...]
    all_to_all x2, waiting for transfers between devices: 14.8 us -> 8.47 us  [refresh(): lax.all_to_all(to_send(query_part, widths[0]), 'tp', split_axis=2, concat...]
    another operation x8 -> x12, local copies, waits for them, and re-layouts: 9.43 us -> 8.41 us
  transfers between devices with their start and end apart: 11 -> 13, of which waited for: 8 -> 11; matrix products, arithmetic and copies ran while one was open for 17% -> 15% of each run, Pallas kernels for 0% -> 0%
where the time goes in v1:
time: 361 us; the launch traced here: 358 us
  blocking collectives  97 us (27%)
  waiting for transfers between devices  81.4 us (23%)
  local copies, waits for them, and re-layouts  80 us (22%)
  starting transfers between devices  79.1 us (22%)
  other arithmetic  14.3 us (4%)
  matrix products  4.92 us (1%)
    all_gather x2, blocking collectives, refresh(): lax.all_gather(key_part, 'tp', axis=3, tiled=True)  68 us
    all_to_all x8, starting transfers between devices, refresh(): lax.all_to_all(for_sending(pieces), 'fsdp', split_axis=1, concat_axis=3,...  49.2 us
    all_to_all x8, waiting for transfers between devices, refresh(): lax.all_to_all(for_sending(pieces), 'fsdp', split_axis=1, concat_axis=3,...  44.2 us
    all_to_all x1, blocking collectives, refresh(): lax.all_to_all(to_send(out_part, widths[3]), 'tp', split_axis=2, concat_a...  29 us
    slice x1, local copies, waits for them, and re-layouts, per_device(): learner_flat[layer_id:layer_id + 1]  28.8 us
    all_to_all x2, waiting for transfers between devices, tiled_gather(): lax.all_to_all(jnp.tile(x, repeats), axis, split_axis=dim, concat_axis=di...  28.8 us
    gather x8, local copies, waits for them, and re-layouts, cut_pieces(): picked = jnp.take_along_axis(row_table, row_ids[:, :, None], axis=1)  18.4 us
    all_to_all x2, starting transfers between devices, refresh(): lax.all_to_all(to_send(query_part, widths[0]), 'tp', split_axis=2, concat...  13.8 us
  transfers between devices with their start and end apart: 13, of which 11 were waited for; matrix products, arithmetic and copies ran while one was open for 15% of the time, Pallas kernels for 0%

profile of v1, /device:TPU:38, one launch (start us, length us, event | category | flops | bytes accessed | tf_op | source)
XLA Modules:
  0.0 358.0 jit_solution(15795769746665352532)
XLA Ops:
  4.4 28.8 %slice_reduce_fusion.1 = (bf16[622592]{0:T(1024)(128)(2,1)S(1)}, bf16[622592]{0:T(1024)(128)(2,1)}) fusion(bf16[2,622592]{1,0:T(2,128)(2,1)} %param.16), kind=kLoop, calls=%fused_computation.18 | loop fusion | bytes 4980736 | tf_op jit(solution)/shard_map/slice | solution.py:119
  35.2 7.6 %all-to-all-start.8 = ((bf16[1,32,4,1,256]{4,2,3,0,1:T(4,128)(2,1)}), bf16[1,32,4,1,256]{4,2,3,0,1:T(4,128)(2,1)S(1)}, u32[]{:S(2)}, u32[]{:S(2)}) async-start(bf16[1,32,4,1,256]{4,2,3,0,1:T(4,128)(2,1)} %bitcast.57), calls=%async_computation.8 | async-start | bytes 131072 | tf_op jit(solution)/shard_map/all_to_all | solution.py:70
  49.2 2.2 reshape.656
  55.6 7.4 %all-to-all-start.2 = ((bf16[1,32,4,1,256]{4,2,3,0,1:T(4,128)(2,1)}), bf16[1,32,4,1,256]{4,2,3,0,1:T(4,128)(2,1)S(1)}, u32[]{:S(2)}, u32[]{:S(2)}) async-start(bf16[1,32,4,1,256]{4,2,3,0,1:T(4,128)(2,1)} %bitcast.18), calls=%async_computation.2 | async-start | bytes 131072 | tf_op jit(solution)/shard_map/all_to_all | solution.py:70
  66.1 2.6 all-to-all-done.2
  68.7 5.6 %all-to-all-start = ((bf16[1,32,4,1,768]{4,2,3,0,1:T(4,128)(2,1)}), bf16[1,32,4,1,768]{4,2,3,0,1:T(4,128)(2,1)S(1)}, u32[]{:S(2)}, u32[]{:S(2)}) async-start(bf16[1,32,4,1,768]{4,2,3,0,1:T(4,128)(2,1)} %bitcast.6), calls=%async_computation | async-start | bytes 393216 | tf_op jit(solution)/shard_map/all_to_all | solution.py:70
  74.3 6.6 %all-to-all-done = bf16[1,32,4,1,768]{4,2,3,0,1:T(4,128)(2,1)S(1)} async-done(((bf16[1,32,4,1,768]{4,2,3,0,1:T(4,128)(2,1)}), bf16[1,32,4,1,768]{4,2,3,0,1:T(4,128)(2,1)S(1)}, u32[]{:S(2)}, u32[]{:S(2)}) %all-to-all-start) | async-done | bytes 196640 | tf_op jit(solution)/shard_map/all_to_all | solution.py:70
  80.9 5.5 %all-to-all-start.3 = ((bf16[1,32,4,1,768]{4,2,3,0,1:T(4,128)(2,1)}), bf16[1,32,4,1,768]{4,2,3,0,1:T(4,128)(2,1)S(1)}, u32[]{:S(2)}, u32[]{:S(2)}) async-start(bf16[1,32,4,1,768]{4,2,3,0,1:T(4,128)(2,1)} %bitcast.28), calls=%async_computation.3 | async-start | bytes 393216 | tf_op jit(solution)/shard_map/all_to_all | solution.py:70
  86.4 6.6 %all-to-all-done.3 = bf16[1,32,4,1,768]{4,2,3,0,1:T(4,128)(2,1)S(1)} async-done(((bf16[1,32,4,1,768]{4,2,3,0,1:T(4,128)(2,1)}), bf16[1,32,4,1,768]{4,2,3,0,1:T(4,128)(2,1)S(1)}, u32[]{:S(2)}, u32[]{:S(2)}) %all-to-all-start.3) | async-done | bytes 196640 | tf_op jit(solution)/shard_map/all_to_all | solution.py:70
  92.9 5.5 %all-to-all-start.12 = ((bf16[1,32,4,1,256]{4,2,3,0,1:T(4,128)(2,1)}), bf16[1,32,4,1,256]{4,2,3,0,1:T(4,128)(2,1)S(1)}, u32[]{:S(2)}, u32[]{:S(2)}) async-start(bf16[1,32,4,1,256]{4,2,3,0,1:T(4,128)(2,1)} %bitcast.75), calls=%async_computation.12 | async-start | bytes 131072 | tf_op jit(solution)/shard_map/all_to_all | solution.py:70
  100.1 4.1 %all-to-all-done.12 = bf16[1,32,4,1,256]{4,2,3,0,1:T(4,128)(2,1)S(1)} async-done(((bf16[1,32,4,1,256]{4,2,3,0,1:T(4,128)(2,1)}), bf16[1,32,4,1,256]{4,2,3,0,1:T(4,128)(2,1)S(1)}, u32[]{:S(2)}, u32[]{:S(2)}) %all-to-all-start.12) | async-done | bytes 65568 | tf_op jit(solution)/shard_map/all_to_all | solution.py:70
  104.1 5.6 %all-to-all-start.5 = ((bf16[1,32,4,1,256]{4,2,3,0,1:T(4,128)(2,1)}), bf16[1,32,4,1,256]{4,2,3,0,1:T(4,128)(2,1)S(1)}, u32[]{:S(2)}, u32[]{:S(2)}) async-start(bf16[1,32,4,1,256]{4,2,3,0,1:T(4,128)(2,1)} %bitcast.40), calls=%async_computation.5 | async-start | bytes 131072 | tf_op jit(solution)/shard_map/all_to_all | solution.py:70
  110.7 4.8 %all-to-all-done.5 = bf16[1,32,4,1,256]{4,2,3,0,1:T(4,128)(2,1)S(1)} async-done(((bf16[1,32,4,1,256]{4,2,3,0,1:T(4,128)(2,1)}), bf16[1,32,4,1,256]{4,2,3,0,1:T(4,128)(2,1)S(1)}, u32[]{:S(2)}, u32[]{:S(2)}) %all-to-all-start.5) | async-done | bytes 65568 | tf_op jit(solution)/shard_map/all_to_all | solution.py:70
  115.5 8.6 %all-to-all-start.1 = ((bf16[1,4,8,4,1,768]{5,3,1,4,0,2:T(4,128)(2,1)}), bf16[1,4,8,4,1,768]{5,3,1,4,0,2:T(4,128)(2,1)}, u32[]{:S(2)}, u32[]{:S(2)}) async-start(bf16[1,4,8,4,1,768]{5,3,1,4,0,2:T(4,128)(2,1)} %get-tuple-element.46), calls=%async_computation.1 | async-start | bytes 393216 | tf_op jit(solution)/shard_map/all_to_all | solution.py:90
  125.9 5.5 %gather_fusion.8 = bf16[1792,256]{1,0:T(8,128)(2,1)S(1)} fusion(bf16[2432,256]{1,0:T(8,128)(2,1)S(1)} %reshape.637, s32[2048]{0:T(1024)S(1)} %pad_clamp_fusion.1), kind=kCustom, calls=%fused_computation.4.clone | custom fusion | bytes 1842176 | tf_op jit(solution)/shard_map/jit(take_along_axis)/gather | solution.py:42
  133.4 5.2 %all-to-all-start.4 = ((bf16[1,4,8,4,1,768]{5,3,1,4,0,2:T(4,128)(2,1)}), bf16[1,4,8,4,1,768]{5,3,1,4,0,2:T(4,128)(2,1)S(1)}, u32[]{:S(2)}, u32[]{:S(2)}) async-start(bf16[1,4,8,4,1,768]{5,3,1,4,0,2:T(4,128)(2,1)} %get-tuple-element.47), calls=%async_computation.4 | async-start | bytes 393216 | tf_op jit(solution)/shard_map/all_to_all | solution.py:90
  140.9 6.4 %all-to-all-done.4 = bf16[1,4,8,4,1,768]{5,3,1,4,0,2:T(4,128)(2,1)S(1)} async-done(((bf16[1,4,8,4,1,768]{5,3,1,4,0,2:T(4,128)(2,1)}), bf16[1,4,8,4,1,768]{5,3,1,4,0,2:T(4,128)(2,1)S(1)}, u32[]{:S(2)}, u32[]{:S(2)}) %all-to-all-start.4) | async-done | bytes 196640 | tf_op jit(solution)/shard_map/all_to_all | solution.py:90
  147.4 5.6 %all-to-all-start.6 = ((bf16[1,32,4,1,3584]{4,2,3,0,1:T(4,128)(2,1)}), bf16[1,32,4,1,3584]{4,2,3,0,1:T(4,128)(2,1)S(1)}, u32[]{:S(2)}, u32[]{:S(2)}) async-start(bf16[1,32,4,1,3584]{4,2,3,0,1:T(4,128)(2,1)} %bitcast.45), calls=%async_computation.6 | async-start | bytes 1835008 | tf_op jit(solution)/shard_map/all_to_all | solution.py:70
  153.1 5.5 %gather_fusion.11 = bf16[1792,256]{1,0:T(8,128)(2,1)S(1)} fusion(bf16[2432,256]{1,0:T(8,128)(2,1)S(1)} %reshape.656, s32[2048]{0:T(1024)S(1)} %pad_clamp_fusion), kind=kCustom, calls=%fused_computation.12.clone | custom fusion | bytes 1842176 | tf_op jit(solution)/shard_map/jit(take_along_axis)/gather | solution.py:42
  160.2 6.2 %all-to-all-done.6 = bf16[1,32,4,1,3584]{4,2,3,0,1:T(4,128)(2,1)S(1)} async-done(((bf16[1,32,4,1,3584]{4,2,3,0,1:T(4,128)(2,1)}), bf16[1,32,4,1,3584]{4,2,3,0,1:T(4,128)(2,1)S(1)}, u32[]{:S(2)}, u32[]{:S(2)}) %all-to-all-start.6) | async-done | bytes 917536 | tf_op jit(solution)/shard_map/all_to_all | solution.py:70
  166.4 6.5 %all-to-all-start.10 = ((bf16[1,32,4,1,3584]{4,2,3,0,1:T(4,128)(2,1)}), bf16[1,32,4,1,3584]{4,2,3,0,1:T(4,128)(2,1)S(1)}, u32[]{:S(2)}, u32[]{:S(2)}) async-start(bf16[1,32,4,1,3584]{4,2,3,0,1:T(4,128)(2,1)} %bitcast.63), calls=%async_computation.10 | async-start | bytes 1835008 | tf_op jit(solution)/shard_map/all_to_all | solution.py:70
  172.9 13.3 %all-to-all-done.10 = bf16[1,32,4,1,3584]{4,2,3,0,1:T(4,128)(2,1)S(1)} async-done(((bf16[1,32,4,1,3584]{4,2,3,0,1:T(4,128)(2,1)}), bf16[1,32,4,1,3584]{4,2,3,0,1:T(4,128)(2,1)S(1)}, u32[]{:S(2)}, u32[]{:S(2)}) %all-to-all-start.10) | async-done | bytes 917536 | tf_op jit(solution)/shard_map/all_to_all | solution.py:70
  187.1 5.5 %all-to-all-start.9 = ((bf16[1,4,32,8,256]{4,2,1,0,3:T(8,128)(2,1)}), bf16[1,4,32,8,256]{4,2,1,0,3:T(8,128)(2,1)}, u32[]{:S(2)}, u32[]{:S(2)}) async-start(bf16[1,4,32,8,256]{4,2,1,0,3:T(8,128)(2,1)} %tile.17), calls=%async_computation.9 | async-start | bytes 1048576 | tf_op jit(solution)/shard_map/all_to_all | solution.py:17
  196.1 13.8 %all-to-all-done.9 = bf16[1,4,32,8,256]{4,2,1,0,3:T(8,128)(2,1)} async-done(((bf16[1,4,32,8,256]{4,2,1,0,3:T(8,128)(2,1)}), bf16[1,4,32,8,256]{4,2,1,0,3:T(8,128)(2,1)}, u32[]{:S(2)}, u32[]{:S(2)}) %all-to-all-start.9) | async-done | bytes 524320 | tf_op jit(solution)/shard_map/all_to_all | solution.py:17
  210.7 5.8 %all-to-all-start.13 = ((bf16[1,4,32,8,256]{4,2,1,0,3:T(8,128)(2,1)}), bf16[1,4,32,8,256]{4,2,1,0,3:T(8,128)(2,1)}, u32[]{:S(2)}, u32[]{:S(2)}) async-start(bf16[1,4,32,8,256]{4,2,1,0,3:T(8,128)(2,1)} %tile.19), calls=%async_computation.13 | async-start | bytes 1048576 | tf_op jit(solution)/shard_map/all_to_all | solution.py:17
  218.3 14.9 %all-to-all-done.13 = bf16[1,4,32,8,256]{4,2,1,0,3:T(8,128)(2,1)} async-done(((bf16[1,4,32,8,256]{4,2,1,0,3:T(8,128)(2,1)}), bf16[1,4,32,8,256]{4,2,1,0,3:T(8,128)(2,1)}, u32[]{:S(2)}, u32[]{:S(2)}) %all-to-all-start.13) | async-done | bytes 524320 | tf_op jit(solution)/shard_map/all_to_all | solution.py:17
  233.2 29.0 %all_to_all.190 = bf16[1,4,8,4,1,3584]{5,3,1,4,0,2:T(4,128)(2,1)S(1)} all-to-all(bf16[1,4,8,4,1,3584]{5,3,1,4,0,2:T(4,128)(2,1)S(1)} %get-tuple-element.44), channel_id=1, replica_groups=mesh['fsdp'=32,'tp'=8] {'tp'}, dimensions={2} | all-to-all | bytes 1835008 | tf_op jit(solution)/shard_map/all_to_all | solution.py:93
  262.2 4.9 %all-to-all-start.11 = ((bf16[1,4,8,4,1,3584]{5,3,1,4,0,2:T(4,128)(2,1)}), bf16[1,4,8,4,1,3584]{5,3,1,4,0,2:T(4,128)(2,1)S(1)}, u32[]{:S(2)}, u32[]{:S(2)}) async-start(bf16[1,4,8,4,1,3584]{5,3,1,4,0,2:T(4,128)(2,1)} %get-tuple-element.45), calls=%async_computation.11 | async-start | bytes 1835008 | tf_op jit(solution)/shard_map/all_to_all | solution.py:93
  267.1 42.6 %all-gather = bf16[1,1,4,32,8,256]{5,3,4,2,1,0:T(8,128)(2,1)S(1)} all-gather(bf16[1,1,4,32,1,256]{5,3,4,2,1,0:T(8,128)(2,1)S(1)} %bitcast.215), channel_id=2, replica_groups=mesh['fsdp'=32,'tp'=8] {'tp'}, dimensions={4}, use_global_device_ids=true | all-gather | bytes 589824 | tf_op jit(solution)/shard_map/all_gather | solution.py:98
  310.2 25.4 %all-gather.1 = bf16[1,1,4,32,8,256]{5,3,4,2,1,0:T(8,128)(2,1)S(1)} all-gather(bf16[1,1,4,32,1,256]{5,3,4,2,1,0:T(8,128)(2,1)S(1)} %bitcast.216), channel_id=3, replica_groups=mesh['fsdp'=32,'tp'=8] {'tp'}, dimensions={4}, use_global_device_ids=true | all-gather | bytes 589824 | tf_op jit(solution)/shard_map/all_gather | solution.py:98
  351.0 2.2 convert_bitcast_fusion
  354.3 3.7 %pad_maximum_fusion = bf16[2,4,896,512]{3,2,1,0:T(8,128)(2,1)} fusion(bf16[1,4,896,512]{3,2,1,0:T(8,128)(2,1)S(1)} %convert_bitcast_fusion, bf16[1,4,896,512]{3,2,1,0:T(8,128)(2,1)S(1)} %convert_bitcast_fusion.1), kind=kLoop, calls=%fused_computation.14 | loop fusion | flops 3670016 | bytes 14680064 | tf_op jit(solution)/shard_map/concatenate | solution.py:127
  (134 shorter events, 53.4 us)
Async XLA Ops:
  0.6 65.3 %copy-start = (s32[32,8]{0,1:T(8,128)S(1)}, s32[32,8]{0,1:T(8,128)}, u32[]{:S(2)}) copy-start(s32[32,8]{0,1:T(8,128)} %param.19) | copy-start | bytes 3076
  35.2 20.4 %all-to-all-start.8 = ((bf16[1,32,4,1,256]{4,2,3,0,1:T(4,128)(2,1)}), bf16[1,32,4,1,256]{4,2,3,0,1:T(4,128)(2,1)S(1)}, u32[]{:S(2)}, u32[]{:S(2)}) async-start(bf16[1,32,4,1,256]{4,2,3,0,1:T(4,128)(2,1)} %bitcast.57), calls=%async_computation.8 | async-start | bytes 131072 | tf_op jit(solution)/shard_map/all_to_all | solution.py:70
  55.6 13.1 %all-to-all-start.2 = ((bf16[1,32,4,1,256]{4,2,3,0,1:T(4,128)(2,1)}), bf16[1,32,4,1,256]{4,2,3,0,1:T(4,128)(2,1)S(1)}, u32[]{:S(2)}, u32[]{:S(2)}) async-start(bf16[1,32,4,1,256]{4,2,3,0,1:T(4,128)(2,1)} %bitcast.18), calls=%async_computation.2 | async-start | bytes 131072 | tf_op jit(solution)/shard_map/all_to_all | solution.py:70
  68.7 12.2 %all-to-all-start = ((bf16[1,32,4,1,768]{4,2,3,0,1:T(4,128)(2,1)}), bf16[1,32,4,1,768]{4,2,3,0,1:T(4,128)(2,1)S(1)}, u32[]{:S(2)}, u32[]{:S(2)}) async-start(bf16[1,32,4,1,768]{4,2,3,0,1:T(4,128)(2,1)} %bitcast.6), calls=%async_computation | async-start | bytes 393216 | tf_op jit(solution)/shard_map/all_to_all | solution.py:70
  74.3 41.2 %copy-start.8 = (pred[8]{0:T(512)(128)(4,1)}, pred[8]{0:T(512)(128)(4,1)S(1)}, u32[]{:S(2)}) copy-start(pred[8]{0:T(512)(128)(4,1)S(1)} %compare_and_fusion) | copy-start | bytes 28
  80.9 12.0 %all-to-all-start.3 = ((bf16[1,32,4,1,768]{4,2,3,0,1:T(4,128)(2,1)}), bf16[1,32,4,1,768]{4,2,3,0,1:T(4,128)(2,1)S(1)}, u32[]{:S(2)}, u32[]{:S(2)}) async-start(bf16[1,32,4,1,768]{4,2,3,0,1:T(4,128)(2,1)} %bitcast.28), calls=%async_computation.3 | async-start | bytes 393216 | tf_op jit(solution)/shard_map/all_to_all | solution.py:70
  92.9 11.2 %all-to-all-start.12 = ((bf16[1,32,4,1,256]{4,2,3,0,1:T(4,128)(2,1)}), bf16[1,32,4,1,256]{4,2,3,0,1:T(4,128)(2,1)S(1)}, u32[]{:S(2)}, u32[]{:S(2)}) async-start(bf16[1,32,4,1,256]{4,2,3,0,1:T(4,128)(2,1)} %bitcast.75), calls=%async_computation.12 | async-start | bytes 131072 | tf_op jit(solution)/shard_map/all_to_all | solution.py:70
  104.1 21.8 %copy-start.4 = (bf16[1,32,4,1,256]{4,2,3,0,1:T(4,128)(2,1)}, bf16[1,32,4,1,256]{4,2,3,0,1:T(4,128)(2,1)S(1)}, u32[]{:S(2)}) copy-start(bf16[1,32,4,1,256]{4,2,3,0,1:T(4,128)(2,1)S(1)} %all-to-all-done.12) | copy-start | bytes 196612
  104.1 11.3 %all-to-all-start.5 = ((bf16[1,32,4,1,256]{4,2,3,0,1:T(4,128)(2,1)}), bf16[1,32,4,1,256]{4,2,3,0,1:T(4,128)(2,1)S(1)}, u32[]{:S(2)}, u32[]{:S(2)}) async-start(bf16[1,32,4,1,256]{4,2,3,0,1:T(4,128)(2,1)} %bitcast.40), calls=%async_computation.5 | async-start | bytes 131072 | tf_op jit(solution)/shard_map/all_to_all | solution.py:70
  115.5 10.5 %copy-start.2 = (bf16[1,32,4,1,256]{4,2,3,0,1:T(4,128)(2,1)}, bf16[1,32,4,1,256]{4,2,3,0,1:T(4,128)(2,1)S(1)}, u32[]{:S(2)}) copy-start(bf16[1,32,4,1,256]{4,2,3,0,1:T(4,128)(2,1)S(1)} %all-to-all-done.5) | copy-start | bytes 196612
  115.5 18.0 %all-to-all-start.1 = ((bf16[1,4,8,4,1,768]{5,3,1,4,0,2:T(4,128)(2,1)}), bf16[1,4,8,4,1,768]{5,3,1,4,0,2:T(4,128)(2,1)}, u32[]{:S(2)}, u32[]{:S(2)}) async-start(bf16[1,4,8,4,1,768]{5,3,1,4,0,2:T(4,128)(2,1)} %get-tuple-element.46), calls=%async_computation.1 | async-start | bytes 393216 | tf_op jit(solution)/shard_map/all_to_all | solution.py:90
  133.4 13.9 %all-to-all-start.4 = ((bf16[1,4,8,4,1,768]{5,3,1,4,0,2:T(4,128)(2,1)}), bf16[1,4,8,4,1,768]{5,3,1,4,0,2:T(4,128)(2,1)S(1)}, u32[]{:S(2)}, u32[]{:S(2)}) async-start(bf16[1,4,8,4,1,768]{5,3,1,4,0,2:T(4,128)(2,1)} %get-tuple-element.47), calls=%async_computation.4 | async-start | bytes 393216 | tf_op jit(solution)/shard_map/all_to_all | solution.py:90
  139.6 13.4 %copy-start.6 = (s32[1,1792,1]{1,2,0:T(1,128)S(1)}, s32[1,1792,1]{1,2,0:T(1,128)}, u32[]{:S(2)}) copy-start(s32[1,1792,1]{1,2,0:T(1,128)} %get-tuple-element.35) | copy-start | bytes 21508
  147.4 19.0 %all-to-all-start.6 = ((bf16[1,32,4,1,3584]{4,2,3,0,1:T(4,128)(2,1)}), bf16[1,32,4,1,3584]{4,2,3,0,1:T(4,128)(2,1)S(1)}, u32[]{:S(2)}, u32[]{:S(2)}) async-start(bf16[1,32,4,1,3584]{4,2,3,0,1:T(4,128)(2,1)} %bitcast.45), calls=%async_computation.6 | async-start | bytes 1835008 | tf_op jit(solution)/shard_map/all_to_all | solution.py:70
  153.1 5.5 %copy-start.7 = (pred[1792]{0:T(1024)(128)(4,1)S(1)}, pred[1792]{0:T(1024)(128)(4,1)}, u32[]{:S(2)}) copy-start(pred[1792]{0:T(1024)(128)(4,1)} %get-tuple-element.34) | copy-start | bytes 5380
  166.4 26.2 %copy-start.5 = (bf16[1,32,4,1,256]{4,2,3,0,1:T(4,128)(2,1)S(1)}, bf16[1,32,4,1,256]{4,2,3,0,1:T(4,128)(2,1)}, u32[]{:S(2)}) copy-start(bf16[1,32,4,1,256]{4,2,3,0,1:T(4,128)(2,1)} %copy-done.4) | copy-start | bytes 196612
  166.4 19.9 %all-to-all-start.10 = ((bf16[1,32,4,1,3584]{4,2,3,0,1:T(4,128)(2,1)}), bf16[1,32,4,1,3584]{4,2,3,0,1:T(4,128)(2,1)S(1)}, u32[]{:S(2)}, u32[]{:S(2)}) async-start(bf16[1,32,4,1,3584]{4,2,3,0,1:T(4,128)(2,1)} %bitcast.63), calls=%async_computation.10 | async-start | bytes 1835008 | tf_op jit(solution)/shard_map/all_to_all | solution.py:70
  187.1 22.7 %all-to-all-start.9 = ((bf16[1,4,32,8,256]{4,2,1,0,3:T(8,128)(2,1)}), bf16[1,4,32,8,256]{4,2,1,0,3:T(8,128)(2,1)}, u32[]{:S(2)}, u32[]{:S(2)}) async-start(bf16[1,4,32,8,256]{4,2,1,0,3:T(8,128)(2,1)} %tile.17), calls=%async_computation.9 | async-start | bytes 1048576 | tf_op jit(solution)/shard_map/all_to_all | solution.py:17
  194.7 21.8 %copy-start.9 = (pred[8]{0:T(512)(128)(4,1)S(1)}, pred[8]{0:T(512)(128)(4,1)}, u32[]{:S(2)}) copy-start(pred[8]{0:T(512)(128)(4,1)} %copy-done.8) | copy-start | bytes 28
  210.7 22.5 %all-to-all-start.13 = ((bf16[1,4,32,8,256]{4,2,1,0,3:T(8,128)(2,1)}), bf16[1,4,32,8,256]{4,2,1,0,3:T(8,128)(2,1)}, u32[]{:S(2)}, u32[]{:S(2)}) async-start(bf16[1,4,32,8,256]{4,2,1,0,3:T(8,128)(2,1)} %tile.19), calls=%async_computation.13 | async-start | bytes 1048576 | tf_op jit(solution)/shard_map/all_to_all | solution.py:17
  262.2 87.1 %all-to-all-start.11 = ((bf16[1,4,8,4,1,3584]{5,3,1,4,0,2:T(4,128)(2,1)}), bf16[1,4,8,4,1,3584]{5,3,1,4,0,2:T(4,128)(2,1)S(1)}, u32[]{:S(2)}, u32[]{:S(2)}) async-start(bf16[1,4,8,4,1,3584]{5,3,1,4,0,2:T(4,128)(2,1)} %get-tuple-element.45), calls=%async_computation.11 | async-start | bytes 1835008 | tf_op jit(solution)/shard_map/all_to_all | solution.py:93
  267.1 43.1 %copy-start.3 = (bf16[1,32,4,1,256]{4,2,3,0,1:T(4,128)(2,1)S(1)}, bf16[1,32,4,1,256]{4,2,3,0,1:T(4,128)(2,1)}, u32[]{:S(2)}) copy-start(bf16[1,32,4,1,256]{4,2,3,0,1:T(4,128)(2,1)} %copy-done.2) | copy-start | bytes 196612
  351.0 2.2 copy-start.1
